TPU v7x, 128 devices: a whole 4x4x4 slice. The times are simulated.
128 devices in a mesh: slab: 16 (over z, y_hi, core), deal: 8 (over x, y_lo).
Axes of the slice: x: 4, y: 4 (y_hi: 2, y_lo: 2; y = y_hi * 2 + y_lo), z: 4, core: 2. Of those that a mesh axis runs over, the one named last changes fastest.
Arguments:
- offsets: float32 [131072, 3, 128], P(('slab', 'deal')), may hold values from -0.5 to 0.5
- velocity: float32 [131072, 3, 128], P(('slab', 'deal')), may hold values from -6 to 6
- affine: float32 [131072, 9, 128], P(('slab', 'deal')), may hold values from -6 to 6
- particle_mass: float32 [131072, 128], P(('slab', 'deal')), may hold values from 0.5 to 2
- cell_in_tile: int32 [131072, 128], P(('slab', 'deal')), may hold values from 0 to 255
- block_tile: int32 [131072], P(('slab', 'deal')), may hold values from 0 to 2047, as said below
- live_blocks: int32 [16, 8], P('slab', 'deal'), may hold values from 512 to 1024, as said below
- send_lists: int32 [16, 8, 2, 16], P('slab', 'deal'), may hold values from 0 to 1023, as said below
- send_counts: int32 [16, 8, 2], P('slab', 'deal'), may hold values from 0 to 16, as said below
Outputs:
- updated_particles: float32 [131072, 15, 128], P(('slab', 'deal'))
- arrivals: float32 [16, 8, 2, 16, 16, 128], P('slab', 'deal')
- grid_velocity: float32 [3, 1024, 8192], P(None, 'slab', 'deal')
Inputs may be any that keep to these rules, and one draw needn't show every extreme that they name: `block_tile`: blocks are sorted by cell: on device (s, d) the tiles never fall along its blocks and lie in [max(d * R - M, 0), min((d + 1) * R + M, 2048)) with R = 256 and M = max(R // 16, 1); some device with d > 0 reaches d * R - M. `live_blocks`: some device has all 1024 blocks live. `send_lists`: the 32 entries of one device's two lists are distinct blocks of that device. `send_counts`: counts toward a slab beyond the ends are zero; some device sends 16 blocks downslope.
All inputs are finite; a program needn't handle non-finite values.
Results may differ from a plain program's by a relative error of at most 0.000073.
Values sent between devices are 32-bit elements; how exact they have to be, the bound alone decides.
No kernel may reach another device: no remote copies, remote signals or barrier semaphores. Data moves between devices by JAX's collectives and lax.ppermute only.
A program may use at most 128 MiB of HBM per device.

v0:
```python
import math

import jax
import jax.numpy as jnp
from jax import lax
from jax.sharding import PartitionSpec as P

PX = 64
PLANE = 8192
TILE = 256


time_step = 0.1
viscosity = 0.2
gravity_pull = (3.0, 0.0, -5.0)


def extended(x, sides, width):
    for axis, dim in sides:
        count, length = (lax.axis_size(axis), x.shape[dim])
        up = [(i, (i + 1) % count) for i in range(count - 1)]
        down = [(j, i) for i, j in up]
        last = lax.slice_in_dim(x, length - width, length, axis=dim)
        initial = lax.slice_in_dim(x, 0, width, axis=dim)
        before = lax.ppermute(last, axis, up)
        after = lax.ppermute(initial, axis, down)
        x = jnp.concatenate([before, x, after], axis=dim)
    return x


def from_behind(x, axis, by):
    count = lax.axis_size(axis)
    pairs = [(i, i + by) for i in range(count) if 0 <= i + by < count]
    return lax.ppermute(x, axis, pairs)


def momentum(offsets, velocity, affine):
    columns = []
    for column in range(3):
        total = velocity[:, column]
        for inner in range(3):
            total = total - affine[:, 3 * column + inner] * offsets[:, inner]
        columns.append(total)
    return jnp.stack(columns, axis=1)


def grid_update(summed):
    floor_mass = jnp.maximum(summed[0], 1.0)
    speeds = []
    for column in range(3):
        speeds.append(summed[1 + column] / floor_mass + time_step * gravity_pull[column])
    return jnp.stack(speeds, axis=0)


def smooth_planes(speed):
    padded = extended(speed, (("slab", 1),), 1)
    return speed + viscosity * (padded[:, 2:] + padded[:, :-2] - 2.0 * speed)


def new_state(offsets, moved):
    shifted = offsets + time_step * moved
    affine_rows = []
    for column in range(3):
        for inner in range(3):
            affine_rows.append(-4.0 * moved[:, column] * offsets[:, inner])
    return jnp.concatenate([shifted, moved, jnp.stack(affine_rows, axis=1)], axis=1)


def body(
    offsets,
    velocity,
    affine,
    particle_mass,
    cell_in_tile,
    block_tile,
    live_blocks,
    send_lists,
    send_counts,
):
    highest = lax.Precision.HIGHEST
    blocks_here = offsets.shape[0]
    deal_count = lax.axis_size("deal")
    deal_index = lax.axis_index("deal")
    tile_count = PX * PLANE // TILE
    active = (jnp.arange(blocks_here, dtype=jnp.int32) < live_blocks[0, 0]).astype(jnp.float32)
    weight = particle_mass * active[:, None]
    moment = momentum(offsets, velocity, affine)
    deposit = jnp.concatenate([weight[:, None, :], weight[:, None, :] * moment], axis=1)
    group_size = math.gcd(blocks_here, 128)
    group_count = blocks_here // group_size
    grouped_deposit = deposit.reshape(group_count, group_size, 4, 128)
    grouped_cells = cell_in_tile.reshape(group_count, group_size, 128)
    grouped_tiles = block_tile.reshape(group_count, group_size)
    tile_slots = jnp.arange(TILE, dtype=jnp.int32)
    tile_labels = jnp.arange(tile_count, dtype=jnp.int32)

    def scatter_group(accumulated, pieces):
        part_deposit, part_cells, part_tiles = pieces
        selector = (part_cells[:, :, None] == tile_slots).astype(jnp.float32)
        per_block = jnp.einsum("bcp,bpk->bck", part_deposit, selector, precision=highest)
        placing = (part_tiles[:, None] == tile_labels).astype(jnp.float32)
        return (
            accumulated + jnp.einsum("bt,bck->ctk", placing, per_block, precision=highest),
            None,
        )

    start_grid = jnp.zeros((4, tile_count, TILE), jnp.float32)
    accumulated, unused = lax.scan(
        scatter_group, start_grid, (grouped_deposit, grouped_cells, grouped_tiles)
    )
    partial_grid = accumulated.reshape(4, PX, PLANE)
    share_width = PLANE // deal_count
    summed = lax.psum(partial_grid, "deal")
    settled = smooth_planes(grid_update(summed))
    own_share = lax.dynamic_slice_in_dim(settled, deal_index * share_width, share_width, 2)
    tiles_view = settled.reshape(3, tile_count, TILE)

    def gather_group(pieces):
        part_cells, part_tiles = pieces
        selector = (part_cells[:, :, None] == tile_slots).astype(jnp.float32)
        chosen = jnp.take(tiles_view, part_tiles, axis=1)
        return jnp.einsum("cbk,bpk->bcp", chosen, selector, precision=highest)

    moved = lax.map(gather_group, (grouped_cells, grouped_tiles)).reshape(blocks_here, 3, 128)
    state = new_state(offsets, moved)
    records = jnp.concatenate([state, particle_mass[:, None, :]], axis=1)
    lists_here = send_lists[0, 0]
    counts_here = send_counts[0, 0]
    mig_slots = lists_here.shape[1]
    leaving = records[lists_here]
    keeping = (jnp.arange(mig_slots, dtype=jnp.int32)[None, :] < counts_here[:, None]).astype(
        jnp.float32
    )
    leaving = leaving * keeping[:, :, None, None]
    from_left = from_behind(leaving[0], "slab", 1)
    from_right = from_behind(leaving[1], "slab", -1)
    arrivals = jnp.stack([from_left, from_right], axis=0)[None, None]
    return (state, arrivals, own_share)


def solution(mesh):
    placed = (
        P(("slab", "deal"), None, None),
        P(("slab", "deal"), None, None),
        P(("slab", "deal"), None, None),
        P(("slab", "deal"), None),
        P(("slab", "deal"), None),
        P(("slab", "deal")),
        P("slab", "deal"),
        P("slab", "deal", None, None),
        P("slab", "deal", None),
    )
    return jax.shard_map(
        body,
        mesh=mesh,
        in_specs=placed,
        out_specs=(
            P(("slab", "deal"), None, None),
            P("slab", "deal", None, None, None, None),
            P(None, "slab", "deal"),
        ),
        check_vma=False,
    )
```

profile of v0, /device:TPU:36, one launch (start us, length us, event | category | flops | bytes accessed | tf_op | source)
XLA Modules:
  0.0 715.3 jit_solution(17750326959352518418)
XLA Ops:
  9.4 2.9 multiply_subtract_fusion.2
  14.9 2.3 pad_maximum_fusion.7
  17.1 127.7 %while.23 = (s32[]{:T(128)}, f32[4,2048,256]{1,2,0:T(8,128)}, f32[8,128,4,128]{3,2,1,0:T(4,128)}, s32[8,128,128]{2,1,0:T(8,128)}, s32[8,128]{1,0:T(8,128)}, /*index=5*/s32[]{:T(128)}, s32[]{:T(128)}) while((s32[]{:T(128)}, f32[4,2048,256]{1,2,0:T(8,128)}, f32[8,128,4,128]{3,2,1,0:T(4,128)}, s32[8,128,128]{2,1,0:T(8,128)}, ...), condition=%wide.region_1.2_spmd.clone, body=%wide.region_0.1_spmd.clone.sunk | while | flops 3431202816 | bytes 18286184 | solution.py:108
  18.7 6.5 fusion.76
  25.1 6.1 bitcast_add_fusion.2
  32.7 6.5 fusion.76
  39.2 8.2 %bitcast_add_fusion.2 = f32[4,2048,256]{1,2,0:T(8,128)} fusion(f32[4,2048,256]{1,2,0:T(8,128)} %get-tuple-element.245, pred[]{:T(512)S(6)} %compare.3, f32[128,4,256]{2,1,0:T(4,128)S(1)} %fusion.76, s32[128]{0:T(128)S(1)} %fusion.77), kind=kOutput, calls=%fused_computation.24.clone.1 | convolution fusion | flops 3225681920 | bytes 17302016 | tf_op jit(solution)/shard_map/while/body/eval_jaxpr/bt,bck->ctk/dot_general | solution.py:103
  49.0 6.5 fusion.76
  55.5 8.2 %bitcast_add_fusion.2 = f32[4,2048,256]{1,2,0:T(8,128)} fusion(f32[4,2048,256]{1,2,0:T(8,128)} %get-tuple-element.245, pred[]{:T(512)S(6)} %compare.3, f32[128,4,256]{2,1,0:T(4,128)S(1)} %fusion.76, s32[128]{0:T(128)S(1)} %fusion.77), kind=kOutput, calls=%fused_computation.24.clone.1 | convolution fusion | flops 3225681920 | bytes 17302016 | tf_op jit(solution)/shard_map/while/body/eval_jaxpr/bt,bck->ctk/dot_general | solution.py:103
  65.2 6.5 fusion.76
  71.7 8.2 %bitcast_add_fusion.2 = f32[4,2048,256]{1,2,0:T(8,128)} fusion(f32[4,2048,256]{1,2,0:T(8,128)} %get-tuple-element.245, pred[]{:T(512)S(6)} %compare.3, f32[128,4,256]{2,1,0:T(4,128)S(1)} %fusion.76, s32[128]{0:T(128)S(1)} %fusion.77), kind=kOutput, calls=%fused_computation.24.clone.1 | convolution fusion | flops 3225681920 | bytes 17302016 | tf_op jit(solution)/shard_map/while/body/eval_jaxpr/bt,bck->ctk/dot_general | solution.py:103
  81.5 6.5 fusion.76
  87.9 8.2 %bitcast_add_fusion.2 = f32[4,2048,256]{1,2,0:T(8,128)} fusion(f32[4,2048,256]{1,2,0:T(8,128)} %get-tuple-element.245, pred[]{:T(512)S(6)} %compare.3, f32[128,4,256]{2,1,0:T(4,128)S(1)} %fusion.76, s32[128]{0:T(128)S(1)} %fusion.77), kind=kOutput, calls=%fused_computation.24.clone.1 | convolution fusion | flops 3225681920 | bytes 17302016 | tf_op jit(solution)/shard_map/while/body/eval_jaxpr/bt,bck->ctk/dot_general | solution.py:103
  97.7 6.5 fusion.76
  104.2 8.2 %bitcast_add_fusion.2 = f32[4,2048,256]{1,2,0:T(8,128)} fusion(f32[4,2048,256]{1,2,0:T(8,128)} %get-tuple-element.245, pred[]{:T(512)S(6)} %compare.3, f32[128,4,256]{2,1,0:T(4,128)S(1)} %fusion.76, s32[128]{0:T(128)S(1)} %fusion.77), kind=kOutput, calls=%fused_computation.24.clone.1 | convolution fusion | flops 3225681920 | bytes 17302016 | tf_op jit(solution)/shard_map/while/body/eval_jaxpr/bt,bck->ctk/dot_general | solution.py:103
  113.9 6.5 fusion.76
  120.4 8.2 %bitcast_add_fusion.2 = f32[4,2048,256]{1,2,0:T(8,128)} fusion(f32[4,2048,256]{1,2,0:T(8,128)} %get-tuple-element.245, pred[]{:T(512)S(6)} %compare.3, f32[128,4,256]{2,1,0:T(4,128)S(1)} %fusion.76, s32[128]{0:T(128)S(1)} %fusion.77), kind=kOutput, calls=%fused_computation.24.clone.1 | convolution fusion | flops 3225681920 | bytes 17302016 | tf_op jit(solution)/shard_map/while/body/eval_jaxpr/bt,bck->ctk/dot_general | solution.py:103
  130.2 6.5 fusion.76
  136.7 8.2 %bitcast_add_fusion.2 = f32[4,2048,256]{1,2,0:T(8,128)} fusion(f32[4,2048,256]{1,2,0:T(8,128)} %get-tuple-element.245, pred[]{:T(512)S(6)} %compare.3, f32[128,4,256]{2,1,0:T(4,128)S(1)} %fusion.76, s32[128]{0:T(128)S(1)} %fusion.77), kind=kOutput, calls=%fused_computation.24.clone.1 | convolution fusion | flops 3225681920 | bytes 17302016 | tf_op jit(solution)/shard_map/while/body/eval_jaxpr/bt,bck->ctk/dot_general | solution.py:103
  144.9 8.7 %copy.94 = f32[4,2048,256]{2,1,0:T(8,128)} copy(f32[4,2048,256]{1,2,0:T(8,128)} %get-tuple-element.72) | data formatting | bytes 16777216 | tf_op jit(solution)/shard_map/while | solution.py:108
  153.6 9.4 %reshape.134 = f32[4,64,8192]{2,1,0:T(8,128)} reshape(f32[4,2048,256]{2,1,0:T(8,128)} %copy.94) | data formatting | bytes 16777216 | tf_op jit(solution)/shard_map/reshape | solution.py:111
  163.8 344.7 %all-reduce.2.cloned.1.call-done = f32[4,64,8192]{2,1,0:T(8,128)} async-done(((f32[4,64,8192]{2,1,0:T(8,128)}), f32[4,64,8192]{2,1,0:T(8,128)}) %all-reduce.2.cloned.1.call-update) | async-done | bytes 8388624 | tf_op jit(solution)/shard_map/psum | solution.py:113
  508.5 4.3 fusion.30
  515.7 6.2 collective-permute-start
  524.4 4.4 fusion.28
  528.8 7.1 reshape.135
  535.8 10.7 %copy.99 = f32[3,2048,256]{2,0,1:T(4,128)} copy(f32[3,2048,256]{2,1,0:T(8,128)} %reshape.135) | data formatting | bytes 12582912
  546.5 130.2 %while.22 = (s32[]{:T(128)}, f32[8,128,3,128]{3,1,0,2:T(8,128)S(1)}, s32[8,128]{1,0:T(8,128)}, f32[3,2048,256]{2,0,1:T(4,128)}, s32[8,128,128]{2,1,0:T(8,128)}, /*index=5*/s32[]{:T(128)}) while((s32[]{:T(128)}, f32[8,128,3,128]{3,1,0,2:T(8,128)S(1)}, s32[8,128]{1,0:T(8,128)}, f32[3,2048,256]{2,0,1:T(4,128)}, ...), condition=%wide.region_4.5_spmd.clone, body=%wide.region_3.4_spmd.clone.sunk | while | flops 155289728 | bytes 2038621 | solution.py:124
  548.9 5.0 gather_fusion
  553.9 8.9 %fusion.72 = f32[1,128,3,128]{3,2,1,0:T(4,128)S(1)} fusion(s32[128,128]{1,0:T(8,128)S(1)} %dynamic-slice_bitcast_fusion.4, f32[128,3,256]{2,1,0:T(4,128)} %gather_fusion, pred[128]{0:T(512)(128)(4,1)S(1)} %compare_and_fusion.2), kind=kOutput, calls=%fused_computation.8.clone.1 | convolution fusion | flops 155287552 | bytes 655488 | tf_op jit(solution)/shard_map/while/body/eval_jaxpr/cbk,bpk->bcp/dot_general | solution.py:122
  565.2 5.0 gather_fusion
  570.2 8.9 %fusion.72 = f32[1,128,3,128]{3,2,1,0:T(4,128)S(1)} fusion(s32[128,128]{1,0:T(8,128)S(1)} %dynamic-slice_bitcast_fusion.4, f32[128,3,256]{2,1,0:T(4,128)} %gather_fusion, pred[128]{0:T(512)(128)(4,1)S(1)} %compare_and_fusion.2), kind=kOutput, calls=%fused_computation.8.clone.1 | convolution fusion | flops 155287552 | bytes 655488 | tf_op jit(solution)/shard_map/while/body/eval_jaxpr/cbk,bpk->bcp/dot_general | solution.py:122
  581.4 5.0 gather_fusion
  586.5 8.9 %fusion.72 = f32[1,128,3,128]{3,2,1,0:T(4,128)S(1)} fusion(s32[128,128]{1,0:T(8,128)S(1)} %dynamic-slice_bitcast_fusion.4, f32[128,3,256]{2,1,0:T(4,128)} %gather_fusion, pred[128]{0:T(512)(128)(4,1)S(1)} %compare_and_fusion.2), kind=kOutput, calls=%fused_computation.8.clone.1 | convolution fusion | flops 155287552 | bytes 655488 | tf_op jit(solution)/shard_map/while/body/eval_jaxpr/cbk,bpk->bcp/dot_general | solution.py:122
  597.7 5.0 gather_fusion
  602.7 8.9 %fusion.72 = f32[1,128,3,128]{3,2,1,0:T(4,128)S(1)} fusion(s32[128,128]{1,0:T(8,128)S(1)} %dynamic-slice_bitcast_fusion.4, f32[128,3,256]{2,1,0:T(4,128)} %gather_fusion, pred[128]{0:T(512)(128)(4,1)S(1)} %compare_and_fusion.2), kind=kOutput, calls=%fused_computation.8.clone.1 | convolution fusion | flops 155287552 | bytes 655488 | tf_op jit(solution)/shard_map/while/body/eval_jaxpr/cbk,bpk->bcp/dot_general | solution.py:122
  613.9 5.0 gather_fusion
  619.0 8.9 %fusion.72 = f32[1,128,3,128]{3,2,1,0:T(4,128)S(1)} fusion(s32[128,128]{1,0:T(8,128)S(1)} %dynamic-slice_bitcast_fusion.4, f32[128,3,256]{2,1,0:T(4,128)} %gather_fusion, pred[128]{0:T(512)(128)(4,1)S(1)} %compare_and_fusion.2), kind=kOutput, calls=%fused_computation.8.clone.1 | convolution fusion | flops 155287552 | bytes 655488 | tf_op jit(solution)/shard_map/while/body/eval_jaxpr/cbk,bpk->bcp/dot_general | solution.py:122
  630.2 5.0 gather_fusion
  635.2 8.9 %fusion.72 = f32[1,128,3,128]{3,2,1,0:T(4,128)S(1)} fusion(s32[128,128]{1,0:T(8,128)S(1)} %dynamic-slice_bitcast_fusion.4, f32[128,3,256]{2,1,0:T(4,128)} %gather_fusion, pred[128]{0:T(512)(128)(4,1)S(1)} %compare_and_fusion.2), kind=kOutput, calls=%fused_computation.8.clone.1 | convolution fusion | flops 155287552 | bytes 655488 | tf_op jit(solution)/shard_map/while/body/eval_jaxpr/cbk,bpk->bcp/dot_general | solution.py:122
  646.5 5.0 gather_fusion
  651.5 8.9 %fusion.72 = f32[1,128,3,128]{3,2,1,0:T(4,128)S(1)} fusion(s32[128,128]{1,0:T(8,128)S(1)} %dynamic-slice_bitcast_fusion.4, f32[128,3,256]{2,1,0:T(4,128)} %gather_fusion, pred[128]{0:T(512)(128)(4,1)S(1)} %compare_and_fusion.2), kind=kOutput, calls=%fused_computation.8.clone.1 | convolution fusion | flops 155287552 | bytes 655488 | tf_op jit(solution)/shard_map/while/body/eval_jaxpr/cbk,bpk->bcp/dot_general | solution.py:122
  662.7 5.0 gather_fusion
  667.8 8.9 %fusion.72 = f32[1,128,3,128]{3,2,1,0:T(4,128)S(1)} fusion(s32[128,128]{1,0:T(8,128)S(1)} %dynamic-slice_bitcast_fusion.4, f32[128,3,256]{2,1,0:T(4,128)} %gather_fusion, pred[128]{0:T(512)(128)(4,1)S(1)} %compare_and_fusion.2), kind=kOutput, calls=%fused_computation.8.clone.1 | convolution fusion | flops 155287552 | bytes 655488 | tf_op jit(solution)/shard_map/while/body/eval_jaxpr/cbk,bpk->bcp/dot_general | solution.py:122
  678.7 3.2 copy-done.3
  681.9 8.1 %copy.101 = f32[1024,16,128]{2,1,0:T(8,128)} copy(f32[1024,16,128]{2,0,1:T(8,128)S(1)} %get-tuple-element.173) | data formatting | bytes 16777216 | tf_op jit(solution)/shard_map/concatenate | solution.py:126
  690.0 3.9 gather_fusion.1
  696.0 6.2 collective-permute-start.3
  (111 shorter events, 50.9 us)
Async XLA Ops:
  7.2 5.8 copy-start.1
  7.2 501.4 %all-reduce.2.cloned.1.call-start = ((), (), s32[]{:S(2)}) async-start(), calls=%async_computation | async-start | bytes 16777216 | tf_op jit(solution)/shard_map/psum | solution.py:113
  163.0 0.7 copy-start.4
  163.0 0.8 copy-start.5
  513.8 9.2 %collective-permute-start.1 = (f32[3,1,8192]{2,0,1:T(4,128)S(1)}, f32[3,1,8192]{2,0,1:T(4,128)S(1)}, u32[]{:S(2)}, u32[]{:S(2)}) collective-permute-start(f32[3,1,8192]{2,0,1:T(4,128)S(1)} %copy.97), channel_id=1, source_target_pairs={{0,8},{8,16},{16,24},{24,32},{32,40},{40,48},{48,56},{56,64},{64,7... | collective-permute-start | bytes 294920 | tf_op jit(solution)/shard_map/ppermute | solution.py:25
  515.7 8.6 %collective-permute-start = (f32[3,1,8192]{2,0,1:T(4,128)S(1)}, f32[3,1,8192]{2,0,1:T(4,128)S(1)}, u32[]{:S(2)}, u32[]{:S(2)}) collective-permute-start(f32[3,1,8192]{2,0,1:T(4,128)S(1)} %copy.95), channel_id=1, source_target_pairs={{8,0},{16,8},{24,16},{32,24},{40,32},{48,40},{56,48},{64,56},{72,6... | collective-permute-start | bytes 294920 | tf_op jit(solution)/shard_map/ppermute | solution.py:26
  546.5 130.2 %copy-start = (f32[1024,3,128]{2,0,1:T(8,128)S(1)}, f32[1024,3,128]{2,0,1:T(8,128)}, u32[]{:S(2)}) copy-start(f32[1024,3,128]{2,0,1:T(8,128)} %param.13) | copy-start | bytes 4718596
  677.5 1.0 copy-start.2
  678.7 3.2 copy-start.3
  694.1 13.6 %collective-permute-start.2 = (f32[16,16,128]{2,1,0:T(8,128)S(1)}, f32[16,16,128]{2,1,0:T(8,128)S(1)}, u32[]{:S(2)}, u32[]{:S(2)}) collective-permute-start(f32[16,16,128]{2,1,0:T(8,128)S(1)} %get-tuple-element.171), channel_id=1, source_target_pairs={{0,8},{8,16},{16,24},{24,32},{32,40},{40,48},{48,56},{56,64},{64,7... | collective-permute-start | bytes 393224 | tf_op jit(solution)/shard_map/ppermute | solution.py:34
  696.0 11.7 %collective-permute-start.3 = (f32[16,16,128]{2,1,0:T(8,128)S(1)}, f32[16,16,128]{2,1,0:T(8,128)S(1)}, u32[]{:S(2)}, u32[]{:S(2)}) collective-permute-start(f32[16,16,128]{2,1,0:T(8,128)S(1)} %get-tuple-element.172), channel_id=1, source_target_pairs={{8,0},{16,8},{24,16},{32,24},{40,32},{48,40},{56,48},{64,56},{72,6... | collective-permute-start | bytes 393224 | tf_op jit(solution)/shard_map/ppermute | solution.py:34
Sparse Core Ops, SparseCore 0:
  163.1 345.3 all-reduce.1
where the time goes:
time: 718 us; the launch traced here: 715 us
  waiting for transfers between devices  347 us (48%)
  matrix products  187 us (26%)
  local copies, waits for them, and re-layouts  115 us (16%)
  other arithmetic  35.2 us (5%)
  starting transfers between devices  16.3 us (2%)
  between operations  15 us (2%)
    psum x1, waiting for transfers between devices, body(): summed = lax.psum(partial_grid, 'deal')  345 us
    dot_general x8, matrix products, gather_group(): return jnp.einsum('cbk,bpk->bcp', chosen, selector, precision=highest)  71.3 us
    dot_general x8, matrix products, scatter_group(): jnp.einsum('bt,bck->ctk', placing, per_block, precision=highest)  63.6 us
    dot_general x8, matrix products, scatter_group(): jnp.einsum('bcp,bpk->bck', part_deposit, selector, precision=highest)  51.9 us
    gather x8, local copies, waits for them, and re-layouts, gather_group(): chosen = jnp.take(tiles_view, part_tiles, axis=1)  40.3 us
    unnamed x14, local copies, waits for them, and re-layouts  15.4 us
  transfers between devices with their start and end apart: 5, of which 3 were waited for; matrix products, arithmetic and copies ran while one was open for 1% of the time, Pallas kernels for 0%

commit v1 on v0

v1 whole, which is shorter than its diff:
```python
import functools

import jax
import jax.numpy as jnp
from jax import lax
from jax.experimental import pallas as pl
from jax.experimental.pallas import tpu as pltpu
from jax.sharding import PartitionSpec as P

time_step = 0.1
viscosity = 0.2
gravity_pull = (3.0, 0.0, -5.0)

LANES = 128
ROWS = 8
PLANE_TILES = 32
SHARE = 256
MARGIN = 16
REACH = MARGIN + PLANE_TILES
EXTENT = SHARE + 2 * REACH
BAND = REACH + MARGIN
MOVED = SHARE + 2 * MARGIN
NB = 1024
STEP = 128
GROUPS = 8
UNIT = 64
MIG = 16


def in_hbm(*arrays):
    return [pltpu.with_memory_space_constraint(x, pltpu.HBM) for x in arrays]


def in_vmem(x):
    return pltpu.with_memory_space_constraint(x, pltpu.VMEM)


def first_block_at(tile_ref, tile):
    def halve(i, span):
        low, high = span
        middle = (low + high) // 2
        below = tile_ref[jnp.minimum(middle, NB - 1)] < tile
        more = low < high
        return (
            jnp.where(more & below, middle + 1, low),
            jnp.where(more & jnp.logical_not(below), middle, high),
        )

    return lax.fori_loop(0, 11, halve, (jnp.int32(0), jnp.int32(NB)))[0]


def deposit_kernel(
    outer, shift_ref, tile_ref, live_ref, off_hbm, vel_hbm, aff_hbm, mass_hbm, cell_hbm,
    *rest,
):
    if outer:
        sums_ref, onward_ref, backward_ref = rest[:3]
        rest = rest[3:]
    else:
        sums_ref = rest[0]
        rest = rest[1:]
    off_ref, vel_ref, aff_ref, mass_ref, cell_ref, second_ref, parts_ref, slots_ref, late_ref, sems = rest
    live = live_ref[0, 0]
    shift = shift_ref[0]
    units = NB // UNIT
    left_end = lax.div(first_block_at(tile_ref, shift + REACH - MARGIN + BAND) + (UNIT - 1), UNIT)
    right_start = jnp.maximum(lax.div(first_block_at(tile_ref, shift + SHARE), UNIT), left_end)

    per = STEP // UNIT
    chunks = NB // STEP

    def copies(chunk):
        rows = pl.ds(pl.multiple_of(chunk * STEP, STEP), STEP)
        return [
            pltpu.make_async_copy(off_hbm.at[:, rows, :], off_ref.at[:, rows, :], sems.at[chunk, 0]),
            pltpu.make_async_copy(vel_hbm.at[:, rows, :], vel_ref.at[:, rows, :], sems.at[chunk, 1]),
            pltpu.make_async_copy(aff_hbm.at[:, rows, :], aff_ref.at[:, rows, :], sems.at[chunk, 2]),
            pltpu.make_async_copy(mass_hbm.at[rows, :], mass_ref.at[rows, :], sems.at[chunk, 3]),
            pltpu.make_async_copy(cell_hbm.at[rows, :], cell_ref.at[rows, :], sems.at[chunk, 4]),
        ]

    def begin(chunk, carry):
        first, last = chunk * per, (chunk + 1) * per
        if outer:
            needed = (first < left_end) | (last > right_start)
        else:
            needed = jnp.maximum(first, left_end) < jnp.minimum(last, right_start)

        @pl.when(needed)
        def _():
            for copy in copies(chunk):
                copy.start()

        return carry

    lax.fori_loop(0, chunks, begin, 0)

    def clear(i, carry):
        nothing = jnp.zeros((8, ROWS, LANES), jnp.float32)
        sums_ref[pl.ds(i * 8, 8)] = nothing
        second_ref[pl.ds(i * 8, 8)] = nothing
        return carry

    lax.fori_loop(0, EXTENT // 8, clear, 0)

    slot_ids = lax.broadcasted_iota(jnp.int32, (LANES, LANES), 0).astype(jnp.bfloat16)
    block_ids = lax.broadcasted_iota(jnp.int32, (8, LANES), 0)
    one = jnp.ones((LANES, LANES), jnp.bfloat16)
    zero = jnp.zeros((LANES, LANES), jnp.bfloat16)
    blank = jnp.zeros((16, LANES), jnp.bfloat16)

    def settle(before):
        for b in range(0, UNIT, 2):
            tile_a = tile_ref[before * UNIT + b] - shift
            tile_b = tile_ref[before * UNIT + b + 1] - shift
            sums_ref[tile_a] = sums_ref[tile_a] + late_ref[b]
            second_ref[tile_b] = second_ref[tile_b] + late_ref[b + 1]

    def clear_late(i, carry):
        late_ref[pl.ds(i * 8, 8)] = jnp.zeros((8, ROWS, LANES), jnp.float32)
        return carry

    lax.fori_loop(0, UNIT // 8, clear_late, 0)

    def unit(v, before):
        if outer:
            i = jnp.where(v < left_end, v, v - left_end + right_start)
        else:
            i = v + left_end
        chunk = lax.div(i, per)
        fresh = chunk * per == i
        if outer:
            fresh = fresh | ((v == left_end) & (chunk * per >= left_end))
        else:
            fresh = fresh | (v == 0)

        @pl.when(fresh)
        def _():
            for copy in copies(chunk):
                copy.wait()

        settle(before)
        for u in range(UNIT // 8):
            base = pl.multiple_of(i * UNIT + u * 8, 8)
            rows = pl.ds(base, 8)
            off = [off_ref[c, rows, :] for c in range(3)]
            weight = jnp.where((block_ids + base) < live, mass_ref[rows, :], 0.0)
            parts = [weight]
            for c in range(3):
                total = vel_ref[c, rows, :]
                for k in range(3):
                    total = total - aff_ref[3 * c + k, rows, :] * off[k]
                parts.append(weight * total)
            cell = cell_ref[rows, :]
            upper = cell >= LANES
            slots_ref[u] = (cell & (LANES - 1)).astype(jnp.float32)
            for c in range(4):
                parts_ref[u, pl.ds(c * 8, 8), :] = jnp.where(upper, 0.0, parts[c])
                parts_ref[u, pl.ds((4 + c) * 8, 8), :] = jnp.where(upper, parts[c], 0.0)

            def prepared(b):
                slot = slots_ref[u, pl.ds(b, 8, stride=0), :]
                slot = jnp.concatenate([slot, slot], axis=0).astype(jnp.bfloat16)
                slot = jnp.concatenate([slot] * 8, axis=0)
                chosen = jnp.where(slot == slot_ids, one, zero)
                part = parts_ref[u, pl.ds(b, 8, stride=8), :]
                high = part.astype(jnp.bfloat16).astype(jnp.float32)
                split = jnp.concatenate([high, part - high], axis=0).astype(jnp.bfloat16)
                return split, chosen

            for b in range(0, 8, 2):
                split_a, chosen_a = prepared(b)
                split_b, chosen_b = prepared(b + 1)
                split = jnp.concatenate(
                    [
                        jnp.concatenate([split_a, blank], axis=1),
                        jnp.concatenate([blank, split_b], axis=1),
                    ],
                    axis=0,
                )
                chosen = jnp.concatenate([chosen_a, chosen_b], axis=1)
                both = lax.dot_general(
                    split, chosen, (((1,), (1,)), ((), ())),
                    preferred_element_type=jnp.float32,
                )
                late_ref[u * 8 + b] = both[:8] + both[8:16]
                late_ref[u * 8 + b + 1] = both[16:24] + both[24:]
        return i

    count = left_end + (units - right_start) if outer else right_start - left_end
    settle(lax.fori_loop(0, count, unit, jnp.int32(0)))

    def join(i, carry):
        rows = pl.ds(i * 8, 8)
        sums_ref[rows] = sums_ref[rows] + second_ref[rows]
        return carry

    lax.fori_loop(0, EXTENT // 8, join, 0)

    if outer:

        def send(i, carry):
            onward_ref[pl.ds(i * 8, 8)] = sums_ref[pl.ds(SHARE + i * 8, 8)]
            backward_ref[pl.ds(i * 8, 8)] = sums_ref[pl.ds(REACH - MARGIN + i * 8, 8)]
            return carry

        lax.fori_loop(0, BAND // 8, send, 0)


def deposit(outer, shift, block_tile, live_blocks, offsets, velocity, affine, particle_mass, cells):
    smem = pl.BlockSpec(memory_space=pltpu.SMEM)
    hbm = pl.BlockSpec(memory_space=pltpu.HBM)
    vmem = pl.BlockSpec(memory_space=pltpu.VMEM)
    shapes = [EXTENT, BAND, BAND] if outer else [EXTENT]
    return pl.pallas_call(
        functools.partial(deposit_kernel, outer),
        in_specs=[smem] * 3 + [hbm] * 5,
        out_specs=[vmem] * len(shapes),
        out_shape=[jax.ShapeDtypeStruct((n, ROWS, LANES), jnp.float32) for n in shapes],
        scratch_shapes=[
            pltpu.VMEM((3, NB, LANES), jnp.float32),
            pltpu.VMEM((3, NB, LANES), jnp.float32),
            pltpu.VMEM((9, NB, LANES), jnp.float32),
            pltpu.VMEM((NB, LANES), jnp.float32),
            pltpu.VMEM((NB, LANES), jnp.int32),
            pltpu.VMEM((EXTENT, ROWS, LANES), jnp.float32),
            pltpu.VMEM((UNIT // 8, 64, LANES), jnp.float32),
            pltpu.VMEM((UNIT // 8, 8, LANES), jnp.float32),
            pltpu.VMEM((UNIT, ROWS, LANES), jnp.float32),
            pltpu.SemaphoreType.DMA((NB // STEP, 5)),
        ],
        compiler_params=pltpu.CompilerParams(vmem_limit_bytes=40 << 20),
        cost_estimate=pl.CostEstimate(
            flops=NB * 16 * LANES * LANES, bytes_accessed=10 << 20, transcendentals=0
        ),
        name="deposit_outer" if outer else "deposit_inner",
    )(shift, block_tile, live_blocks, *in_hbm(offsets, velocity, affine, particle_mass, cells))


def gather_blocks(tiles_of, row_of, moved_ref, found_ref, cell_ref, base, slot):
    for b in range(8):
        place = row_of(b)
        index = cell_ref[pl.ds(base + b, 8, stride=0), :] & (LANES - 1)
        found_ref[slot, pl.ds(b * 8, 8), :] = jnp.take_along_axis(
            moved_ref[place], index, axis=1
        )
    upper = cell_ref[pl.ds(base, 8), :] >= LANES
    return [
        jnp.where(
            upper,
            found_ref[slot, pl.ds(5 + c, 8, stride=8), :],
            found_ref[slot, pl.ds(1 + c, 8, stride=8), :],
        )
        for c in range(3)
    ]


def state_of(off, vel):
    state = [off[c] + time_step * vel[c] for c in range(3)] + list(vel)
    for c in range(3):
        scaled = -4.0 * vel[c]
        for k in range(3):
            state.append(scaled * off[k])
    return state


def grid_kernel(
    shift_ref, ends_ref, tile_ref, list_ref, count_ref,
    sums_ref, inner_ref, left_ref, right_ref, off_ref, mass_ref, cell_ref,
    moved_ref, share_ref, onward_ref, backward_ref,
    total_ref, speed_ref, flat_ref, pick_ref, pick_cell_ref, found_ref,
):
    row_ids = lax.broadcasted_iota(jnp.int32, (ROWS, LANES), 0)
    lower_half = row_ids < 4
    channel = row_ids & 3
    pull = jnp.where(
        channel == 1,
        time_step * gravity_pull[0],
        jnp.where(channel == 3, time_step * gravity_pull[2], time_step * gravity_pull[1]),
    ).astype(jnp.float32)

    def rows_of(j):
        return pl.ds(pl.multiple_of(j * ROWS, ROWS), ROWS)

    def load_left(j):
        total_ref[rows_of(j), :] = sums_ref[j] + inner_ref[j] + left_ref[j]

    def load_middle(j):
        total_ref[rows_of(j), :] = sums_ref[j] + inner_ref[j]

    def load_right(j):
        total_ref[rows_of(j), :] = sums_ref[j] + inner_ref[j] + right_ref[j - (EXTENT - BAND)]

    def over(first, count, body, unroll=8):
        def some(i, carry):
            for u in range(unroll):
                body(first + i * unroll + u)
            return carry

        lax.fori_loop(0, count // unroll, some, 0)

    over(0, BAND, load_left)
    over(BAND, EXTENT - 2 * BAND, load_middle)
    over(EXTENT - BAND, BAND, load_right)

    def speeds(j):
        total = total_ref[rows_of(j), :]
        mass = jnp.where(
            lower_half,
            total_ref[pl.ds(j * ROWS, ROWS, stride=0), :],
            total_ref[pl.ds(j * ROWS + 4, ROWS, stride=0), :],
        )
        speed_ref[j] = total / jnp.maximum(mass, 1.0) + pull

    over(0, EXTENT, speeds)

    @pl.when(ends_ref[0] == 1)
    def _():
        def none(j):
            speed_ref[j] = jnp.zeros((ROWS, LANES), jnp.float32)

        over(0, REACH, none)

    @pl.when(ends_ref[0] == 2)
    def _():
        def none(j):
            speed_ref[j] = jnp.zeros((ROWS, LANES), jnp.float32)

        over(EXTENT - REACH, REACH, none)

    def smooth(j):
        here = speed_ref[j + PLANE_TILES]
        settled = here + viscosity * (
            speed_ref[j + 2 * PLANE_TILES] + speed_ref[j] - 2.0 * here
        )
        moved_ref[j] = settled
        flat_ref[rows_of(j), :] = settled

    over(0, MOVED, smooth)

    planes = SHARE // PLANE_TILES
    for dest in range(8):
        for c in range(3):
            for q in range(8):
                tile = MARGIN + 4 * dest + q // 2
                start = tile * ROWS + (q % 2) * 4 + 1 + c
                share_ref[dest, c, :, pl.ds(q * LANES, LANES)] = flat_ref[
                    pl.ds(start, planes, stride=PLANE_TILES * ROWS), :
                ]

    shift = shift_ref[0]
    for side, leave_ref in enumerate((onward_ref, backward_ref)):
        for first in range(0, MIG, 8):
            blocks = [list_ref[0, 0, side, first + b] for b in range(8)]
            for b in range(8):
                row = pl.ds(blocks[b], 1)
                for c in range(3):
                    pick_ref[c, pl.ds(b, 1), :] = off_ref[c, row, :]
                pick_ref[3, pl.ds(b, 1), :] = mass_ref[row, :]
                pick_cell_ref[pl.ds(b, 1), :] = cell_ref[row, :]
            vel = gather_blocks(
                None, lambda b: tile_ref[blocks[b]] - shift, moved_ref, found_ref,
                pick_cell_ref, 0, 0,
            )
            off = [pick_ref[c] for c in range(3)]
            record = state_of(off, vel) + [pick_ref[3]]
            keep = (row_ids + first) < count_ref[0, 0, side]
            for c in range(16):
                rows = pl.ds(first * 16 + c, 8, stride=16)
                leave_ref[rows, :] = jnp.where(keep, record[c], 0.0)


def grid_step(shift, ends, block_tile, lists, counts, sums, inner, left, right, offsets, mass, cells):
    smem = pl.BlockSpec(memory_space=pltpu.SMEM)
    vmem = pl.BlockSpec(memory_space=pltpu.VMEM)
    planes = SHARE // PLANE_TILES
    return pl.pallas_call(
        grid_kernel,
        in_specs=[smem] * 5 + [vmem] * 7,
        out_specs=[vmem] * 4,
        out_shape=[
            jax.ShapeDtypeStruct((MOVED, ROWS, LANES), jnp.float32),
            jax.ShapeDtypeStruct((8, 3, planes, 8 * LANES), jnp.float32),
            jax.ShapeDtypeStruct((MIG * 16, LANES), jnp.float32),
            jax.ShapeDtypeStruct((MIG * 16, LANES), jnp.float32),
        ],
        scratch_shapes=[
            pltpu.VMEM((EXTENT * ROWS, LANES), jnp.float32),
            pltpu.VMEM((EXTENT, ROWS, LANES), jnp.float32),
            pltpu.VMEM((MOVED * ROWS, LANES), jnp.float32),
            pltpu.VMEM((4, 8, LANES), jnp.float32),
            pltpu.VMEM((8, LANES), jnp.int32),
            pltpu.VMEM((1, 64, LANES), jnp.float32),
        ],
        compiler_params=pltpu.CompilerParams(vmem_limit_bytes=24 << 20),
        cost_estimate=pl.CostEstimate(flops=1 << 22, bytes_accessed=8 << 20, transcendentals=0),
        name="grid_step",
    )(shift, ends, block_tile, lists, counts, sums, inner, left, right, offsets, mass, cells)


def update_kernel(shift_ref, tile_ref, moved_ref, off_ref, cell_ref, state_ref, found_ref):
    step = pl.program_id(0)
    shift = shift_ref[0]

    def group(i, carry):
        for u in range(GROUPS):
            base = pl.multiple_of((i * GROUPS + u) * 8, 8)
            rows = pl.ds(base, 8)
            vel = gather_blocks(
                None, lambda b: tile_ref[step * STEP + base + b] - shift, moved_ref,
                found_ref, cell_ref, base, u,
            )
            off = [off_ref[c, rows, :] for c in range(3)]
            state = state_of(off, vel)
            for c in range(15):
                state_ref[c, rows, :] = state[c]
        return carry

    lax.fori_loop(0, STEP // (8 * GROUPS), group, 0)


def update(shift, block_tile, moved, offsets, cells):
    smem = pl.BlockSpec(memory_space=pltpu.SMEM)
    return pl.pallas_call(
        update_kernel,
        grid=(NB // STEP,),
        in_specs=[
            smem,
            smem,
            pl.BlockSpec((MOVED, ROWS, LANES), lambda i: (0, 0, 0)),
            pl.BlockSpec((3, STEP, LANES), lambda i: (0, i, 0)),
            pl.BlockSpec((STEP, LANES), lambda i: (i, 0)),
        ],
        out_specs=pl.BlockSpec((15, STEP, LANES), lambda i: (0, i, 0)),
        out_shape=jax.ShapeDtypeStruct((15, NB, LANES), jnp.float32),
        scratch_shapes=[pltpu.VMEM((GROUPS, 64, LANES), jnp.float32)],
        compiler_params=pltpu.CompilerParams(vmem_limit_bytes=16 << 20),
        cost_estimate=pl.CostEstimate(flops=1 << 22, bytes_accessed=12 << 20, transcendentals=0),
        name="update",
    )(shift, block_tile, in_vmem(moved), *in_hbm(offsets, cells))


def body(
    offsets, velocity, affine, particle_mass, cell_in_tile, block_tile, live_blocks,
    send_lists, send_counts,
):
    deals, slabs = lax.axis_size("deal"), lax.axis_size("slab")
    deal, slab = lax.axis_index("deal"), lax.axis_index("slab")
    place = slab * deals + deal
    off = jnp.transpose(offsets, (1, 0, 2))
    vel = jnp.transpose(velocity, (1, 0, 2))
    aff = jnp.transpose(affine, (1, 0, 2))
    wide = (deal * SHARE - REACH).astype(jnp.int32).reshape(1)
    near = (deal * SHARE - MARGIN).astype(jnp.int32).reshape(1)
    ends = jnp.where(place == 0, 1, jnp.where(place == slabs * deals - 1, 2, 0))
    ends = ends.astype(jnp.int32).reshape(1)
    particles = (wide, block_tile, live_blocks, off, vel, aff, particle_mass, cell_in_tile)
    sums, to_next, to_last = deposit(True, *particles)
    count = slabs * deals
    onward = [(i, i + 1) for i in range(count - 1)]
    backward = [(j, i) for i, j in onward]
    axes = ("slab", "deal")
    left = lax.ppermute(to_next, axes, onward)
    right = lax.ppermute(to_last, axes, backward)
    inner, = deposit(False, *particles)
    moved, share, ahead, behind = grid_step(
        near, ends, block_tile, send_lists, send_counts, sums, inner, left, right, off,
        particle_mass, cell_in_tile,
    )
    ahead, behind = [x.reshape(MIG, 16, LANES) for x in (ahead, behind)]
    down = [(i, i + 1) for i in range(slabs - 1)]
    up = [(j, i) for i, j in down]
    from_left = lax.ppermute(ahead, "slab", down)
    from_right = lax.ppermute(behind, "slab", up)
    own = lax.all_to_all(share, "deal", 0, 0, tiled=True)
    state = update(near, block_tile, moved, off, cell_in_tile)
    arrivals = jnp.stack([from_left, from_right], axis=0)[None, None]
    own = jnp.transpose(own, (1, 0, 2, 3)).reshape(3, deals * (SHARE // PLANE_TILES), 8 * LANES)
    return jnp.transpose(state, (1, 0, 2)), arrivals, own


def solution(mesh):
    both = ("slab", "deal")
    placed = (
        P(both, None, None),
        P(both, None, None),
        P(both, None, None),
        P(both, None),
        P(both, None),
        P(both),
        P("slab", "deal"),
        P("slab", "deal", None, None),
        P("slab", "deal", None),
    )
    return jax.shard_map(
        body,
        mesh=mesh,
        in_specs=placed,
        out_specs=(
            P(both, None, None),
            P("slab", "deal", None, None, None, None),
            P(None, "slab", "deal"),
        ),
        check_vma=False,
    )
```

time: 718 us -> 59.6 us (0.08)
  waiting for transfers between devices: 347 us -> 0.01 us
  matrix products: 187 us -> 0 us
  local copies, waits for them, and re-layouts: 115 us -> 2.66 us
  other arithmetic: 35.2 us -> 0.72 us
  Pallas kernels: 0 us -> 32.4 us
  between operations: 15 us -> 1.47 us
    psum x1 -> x0, waiting for transfers between devices: 345 us -> none  [body(): summed = lax.psum(partial_grid, 'deal')]
    dot_general x24 -> x0, matrix products: 187 us -> none  [the longest x8 71.3 us: gather_group(): return jnp.einsum('cbk,bpk->bcp', chosen, selector, precision=highest)]
    gather x9 -> x0, local copies, waits for them, and re-layouts: 44.2 us -> none  [the longest x8 40.3 us: gather_group(): chosen = jnp.take(tiles_view, part_tiles, axis=1)]
    pallas_call x0 -> x4, Pallas kernels: none -> 32.4 us  [the longest x2 19.9 us: deposit(): pl.pallas_call(functools.partial(deposit_kernel, outer), in_specs=[smem]...]
    eq x24 -> x0, local copies, waits for them, and re-layouts: 19.1 us -> none  [the longest x8 6.8 us: gather_group(): selector = (part_cells[:, :, None] == tile_slots).astype(jnp.float32)]
    reshape x2 -> x1, local copies, waits for them, and re-layouts: 16.4 us -> 0.93 us  [body(): jnp.transpose(own, (1, 0, 2, 3))]
    unnamed x14 -> x18, local copies, waits for them, and re-layouts: 15.4 us -> 1.73 us
    while x1 -> x0, local copies, waits for them, and re-layouts: 8.72 us -> none  [body(): lax.scan(scatter_group, start_grid, (grouped_deposit, grouped_cells, grou...]
  transfers between devices with their start and end apart: 5 -> 5, of which waited for: 3 -> 0; matrix products, arithmetic and copies ran while one was open for 1% -> 1% of each run, Pallas kernels for 0% -> 32%
where the time goes in v1:
time: 59.6 us; the launch traced here: 59.1 us
  Pallas kernels  32.4 us (54%)
  starting transfers between devices  21.9 us (37%)
  local copies, waits for them, and re-layouts  2.66 us (4%)
  between operations  1.47 us (2%)
  other arithmetic  0.72 us (1%)
    pallas_call x2, Pallas kernels, deposit(): pl.pallas_call(functools.partial(deposit_kernel, outer), in_specs=[smem]...  19.9 us
    pallas_call x1, Pallas kernels, update(): pl.pallas_call(update_kernel, grid=(NB // STEP,), in_specs=[smem, smem, p...  8.82 us
    all_to_all x1, starting transfers between devices, body(): own = lax.all_to_all(share, 'deal', 0, 0, tiled=True)  7.17 us
    ppermute x1, starting transfers between devices, body(): from_right = lax.ppermute(behind, 'slab', up)  6.05 us
    pallas_call x1, Pallas kernels, grid_step(): pl.pallas_call(grid_kernel, in_specs=[smem] * 5 + [vmem] * 7, out_specs=[...  3.65 us
    ppermute x1, starting transfers between devices, body(): left = lax.ppermute(to_next, axes, onward)  3.48 us
    ppermute x1, starting transfers between devices, body(): right = lax.ppermute(to_last, axes, backward)  3.26 us
    ppermute x1, starting transfers between devices, body(): from_left = lax.ppermute(ahead, 'slab', down)  1.91 us
  transfers between devices with their start and end apart: 5, of which 0 were waited for; matrix products, arithmetic and copies ran while one was open for 1% of the time, Pallas kernels for 32%

profile of v1, /device:TPU:36, one launch (start us, length us, event | category | flops | bytes accessed | tf_op | source)
XLA Modules:
  0.0 59.1 jit_solution(14699028475686183880)
XLA Ops:
  1.3 0.0 copy-start.5
  1.3 0.7 %copy-done.5 = s32[1024]{0:T(1024)S(1)} copy-done((s32[1024]{0:T(1024)S(1)}, s32[1024]{0:T(1024)}, u32[]{:S(2)}) %copy-start.5) | copy-done | bytes 4120
  2.0 0.0 copy-start.6
  2.0 10.0 %deposit_outer.1 = (f32[352,8,128]{2,1,0:T(8,128)S(1)}, f32[64,8,128]{2,1,0:T(8,128)S(1)}, f32[64,8,128]{2,1,0:T(8,128)S(1)}) custom-call(s32[1]{0:T(128)} %bitcast.2.shift_ref, s32[1024]{0:T(1024)S(1)} %copy-done.5, s32[1,1]{1,0:T(1,128)S(6)} %copy.14.live_ref, f32[3,1024,128]{2,1,0:T(8,128)} %bitcast.18, f32[3,1024,128]{2,1,0:T(8,128)} %bitcast.27, ...), custom_call_target="tpu_custom_call" | custom-call | flops 268435456 | bytes 10485760 | tf_op jit(solution)/shard_map/deposit_outer/pallas_call | solution.py:215
  12.0 3.5 %collective-permute-start = (f32[64,8,128]{2,1,0:T(8,128)S(1)}, f32[64,8,128]{2,1,0:T(8,128)S(1)}, u32[]{:S(2)}, u32[]{:S(2)}) collective-permute-start(f32[64,8,128]{2,1,0:T(8,128)S(1)} %get-tuple-element.11), channel_id=1, source_target_pairs={{0,1},{1,2},{2,3},{3,4},{4,5},{5,6},{6,7},{7,8},{8,9},{9,10},{10,1... | collective-permute-start | bytes 786440 | tf_op jit(solution)/shard_map/ppermute | solution.py:463
  15.4 3.3 %collective-permute-start.1 = (f32[64,8,128]{2,1,0:T(8,128)S(1)}, f32[64,8,128]{2,1,0:T(8,128)S(1)}, u32[]{:S(2)}, u32[]{:S(2)}) collective-permute-start(f32[64,8,128]{2,1,0:T(8,128)S(1)} %get-tuple-element.12), channel_id=1, source_target_pairs={{1,0},{2,1},{3,2},{4,3},{5,4},{6,5},{7,6},{8,7},{9,8},{10,9},{11,1... | collective-permute-start | bytes 786440 | tf_op jit(solution)/shard_map/ppermute | solution.py:464
  18.7 0.0 copy-done.6
  18.7 0.0 copy-start
  18.7 0.0 copy-start.1
  18.8 0.0 copy-start.2
  18.8 0.0 copy-start.7
  18.8 0.0 copy-start.8
  18.8 9.9 %deposit_inner.1.inner_ref = f32[352,8,128]{2,1,0:T(8,128)S(1)} custom-call(s32[1]{0:T(128)} %bitcast.2.shift_ref, s32[1024]{0:T(1024)S(1)} %copy-done.6, s32[1,1]{1,0:T(1,128)S(6)} %copy.14.live_ref, f32[3,1024,128]{2,1,0:T(8,128)} %bitcast.19, f32[3,1024,128]{2,1,0:T(8,128)} %bitcast.28, f32[9,1024,128]{2,1,0:T(8,128)} %bitcast.25, f32[1024,128]{1,0:T(8,128)} %mass_ref.1, ...), custom_call_target="tpu_custom_call" | custom-call | flops 268435456 | bytes 10485760 | tf_op jit(solution)/shard_map/deposit_inner/pallas_call | solution.py:215
  28.7 0.0 collective-permute-done.left_ref
  28.7 0.0 collective-permute-done.1.right_ref
  28.7 0.0 copy-done
  28.7 0.0 copy-done.1
  28.8 0.0 copy-done.2
  28.8 0.0 copy-done.7
  28.8 0.0 copy-done.8
  28.8 3.6 %grid_step.1 = (f32[288,8,128]{2,1,0:T(8,128)S(1)}, f32[8,3,8,1024]{3,2,1,0:T(8,128)}, f32[256,128]{1,0:T(8,128)S(1)}, f32[256,128]{1,0:T(8,128)S(1)}) custom-call(s32[1]{0:T(128)} %bitcast.shift_ref, s32[1]{0:T(128)} %bitcast.1.ends_ref, s32[1024]{0:T(1024)S(1)} %copy-done.6, s32[1,1,2,16]{3,2,1,0:T(2,128)S(1)} %copy-done.7, s32[1,1,2]{2,1,0:T(1,128)S(1)} %copy-done.8, ...), custom_call_target="tpu_custom_call" | custom-call | flops 4194304 | bytes 8388608 | tf_op jit(solution)/shard_map/grid_step/pallas_call | solution.py:377
  32.4 0.0 copy-start.3
  32.4 1.0 %copy-done.3 = f32[288,8,128]{2,1,0:T(8,128)} copy-done((f32[288,8,128]{2,1,0:T(8,128)}, f32[288,8,128]{2,1,0:T(8,128)S(1)}, u32[]{:S(2)}) %copy-start.3) | copy-done | bytes 1179672
  33.4 0.0 copy-start.4
  33.4 7.2 %all-to-all-start = ((f32[8,3,8,1024]{3,2,1,0:T(8,128)}), f32[8,3,8,1024]{3,2,1,0:T(8,128)S(1)}, u32[]{:S(2)}, u32[]{:S(2)}) async-start(f32[8,3,8,1024]{3,2,1,0:T(8,128)} %get-tuple-element.16), calls=%async_computation | async-start | bytes 1572864 | tf_op jit(solution)/shard_map/all_to_all | solution.py:475
  40.6 1.9 %collective-permute-start.2 = (f32[16,16,128]{2,1,0:T(8,128)S(1)}, f32[16,16,128]{2,1,0:T(8,128)S(1)}, u32[]{:S(2)}, u32[]{:S(2)}) collective-permute-start(f32[16,16,128]{2,1,0:T(8,128)S(1)} %bitcast.23), channel_id=1, source_target_pairs={{0,8},{8,16},{16,24},{24,32},{32,40},{40,48},{48,56},{56,64},{64,7... | collective-permute-start | bytes 393224 | tf_op jit(solution)/shard_map/ppermute | solution.py:473
  42.5 6.0 %collective-permute-start.3 = (f32[16,16,128]{2,1,0:T(8,128)S(1)}, f32[16,16,128]{2,1,0:T(8,128)S(1)}, u32[]{:S(2)}, u32[]{:S(2)}) collective-permute-start(f32[16,16,128]{2,1,0:T(8,128)S(1)} %bitcast.22), channel_id=1, source_target_pairs={{8,0},{16,8},{24,16},{32,24},{40,32},{48,40},{56,48},{64,56},{72,6... | collective-permute-start | bytes 393224 | tf_op jit(solution)/shard_map/ppermute | solution.py:474
  48.6 0.0 copy-done.4
  48.6 8.8 %update.1 = f32[15,1024,128]{2,1,0:T(8,128)} custom-call(s32[1]{0:T(128)} %bitcast.shift_ref, s32[1024]{0:T(1024)S(1)} %copy-done.6, f32[288,8,128]{2,1,0:T(8,128)S(1)} %copy-done.4, f32[3,1024,128]{2,1,0:T(8,128)} %bitcast.20, s32[1024,128]{1,0:T(8,128)} %cell_ref.3), custom_call_target="tpu_custom_call" | custom-call | flops 4194304 | bytes 12582912 | tf_op jit(solution)/shard_map/update/pallas_call | solution.py:424
  57.4 0.0 collective-permute-done.2
  57.4 0.0 collective-permute-done.3
  57.4 0.7 %maximum_bitcast_fusion = f32[1,1,2,16,16,128]{5,4,3,2,1,0:T(8,128)} fusion(f32[1,16,16,128]{3,2,1,0:T(8,128)S(1)} %bitcast.30, f32[1,16,16,128]{3,2,1,0:T(8,128)S(1)} %bitcast.29), kind=kLoop, calls=%fused_computation.1 | loop fusion | flops 65536 | bytes 524288 | tf_op jit(solution)/shard_map/broadcast_in_dim | solution.py:477
  58.2 0.0 all-to-all-done
  58.2 0.9 %copy_bitcast_fusion = f32[3,64,1024]{2,1,0:T(8,128)} fusion(f32[8,3,8,1024]{3,2,1,0:T(8,128)S(1)} %all-to-all-done), kind=kLoop, calls=%fused_computation | loop fusion | bytes 1572864 | tf_op jit(solution)/shard_map/reshape | solution.py:478
Async XLA Ops:
  1.3 0.7 %copy-start.5 = (s32[1024]{0:T(1024)S(1)}, s32[1024]{0:T(1024)}, u32[]{:S(2)}) copy-start(s32[1024]{0:T(1024)} %tile_ref.7) | copy-start | bytes 12292
  2.0 16.8 %copy-start.6 = (s32[1024]{0:T(1024)S(1)}, s32[1024]{0:T(1024)}, u32[]{:S(2)}) copy-start(s32[1024]{0:T(1024)} %tile_ref.7) | copy-start | bytes 12292
  12.0 16.8 %collective-permute-start = (f32[64,8,128]{2,1,0:T(8,128)S(1)}, f32[64,8,128]{2,1,0:T(8,128)S(1)}, u32[]{:S(2)}, u32[]{:S(2)}) collective-permute-start(f32[64,8,128]{2,1,0:T(8,128)S(1)} %get-tuple-element.11), channel_id=1, source_target_pairs={{0,1},{1,2},{2,3},{3,4},{4,5},{5,6},{6,7},{7,8},{8,9},{9,10},{10,1... | collective-permute-start | bytes 786440 | tf_op jit(solution)/shard_map/ppermute | solution.py:463
  15.4 13.3 %collective-permute-start.1 = (f32[64,8,128]{2,1,0:T(8,128)S(1)}, f32[64,8,128]{2,1,0:T(8,128)S(1)}, u32[]{:S(2)}, u32[]{:S(2)}) collective-permute-start(f32[64,8,128]{2,1,0:T(8,128)S(1)} %get-tuple-element.12), channel_id=1, source_target_pairs={{1,0},{2,1},{3,2},{4,3},{5,4},{6,5},{7,6},{8,7},{9,8},{10,9},{11,1... | collective-permute-start | bytes 786440 | tf_op jit(solution)/shard_map/ppermute | solution.py:464
  18.7 10.0 %copy-start = (f32[1024,3,128]{2,0,1:T(8,128)S(1)}, f32[1024,3,128]{2,0,1:T(8,128)}, u32[]{:S(2)}) copy-start(f32[1024,3,128]{2,0,1:T(8,128)} %param.9) | copy-start | bytes 4718596
  18.7 10.0 %copy-start.1 = (s32[1024,128]{1,0:T(8,128)S(1)}, s32[1024,128]{1,0:T(8,128)}, u32[]{:S(2)}) copy-start(s32[1024,128]{1,0:T(8,128)} %cell_ref.3) | copy-start | bytes 1572868
  18.8 10.0 %copy-start.2 = (f32[1024,128]{1,0:T(8,128)S(1)}, f32[1024,128]{1,0:T(8,128)}, u32[]{:S(2)}) copy-start(f32[1024,128]{1,0:T(8,128)} %mass_ref.1) | copy-start | bytes 1572868
  18.8 10.0 %copy-start.7 = (s32[1,1,2,16]{3,2,1,0:T(2,128)S(1)}, s32[1,1,2,16]{3,2,1,0:T(2,128)}, u32[]{:S(2)}) copy-start(s32[1,1,2,16]{3,2,1,0:T(2,128)} %list_ref.1) | copy-start | bytes 388
  18.8 10.0 %copy-start.8 = (s32[1,1,2]{2,1,0:T(1,128)S(1)}, s32[1,1,2]{2,1,0:T(1,128)}, u32[]{:S(2)}) copy-start(s32[1,1,2]{2,1,0:T(1,128)} %count_ref.1) | copy-start | bytes 28
  32.4 1.0 %copy-start.3 = (f32[288,8,128]{2,1,0:T(8,128)}, f32[288,8,128]{2,1,0:T(8,128)S(1)}, u32[]{:S(2)}) copy-start(f32[288,8,128]{2,1,0:T(8,128)S(1)} %get-tuple-element.13.moved_ref) | copy-start | bytes 3538948
  33.4 15.1 %copy-start.4 = (f32[288,8,128]{2,1,0:T(8,128)S(1)}, f32[288,8,128]{2,1,0:T(8,128)}, u32[]{:S(2)}) copy-start(f32[288,8,128]{2,1,0:T(8,128)} %copy-done.3) | copy-start | bytes 3538948
  33.4 24.7 %all-to-all-start = ((f32[8,3,8,1024]{3,2,1,0:T(8,128)}), f32[8,3,8,1024]{3,2,1,0:T(8,128)S(1)}, u32[]{:S(2)}, u32[]{:S(2)}) async-start(f32[8,3,8,1024]{3,2,1,0:T(8,128)} %get-tuple-element.16), calls=%async_computation | async-start | bytes 1572864 | tf_op jit(solution)/shard_map/all_to_all | solution.py:475
  40.6 16.8 %collective-permute-start.2 = (f32[16,16,128]{2,1,0:T(8,128)S(1)}, f32[16,16,128]{2,1,0:T(8,128)S(1)}, u32[]{:S(2)}, u32[]{:S(2)}) collective-permute-start(f32[16,16,128]{2,1,0:T(8,128)S(1)} %bitcast.23), channel_id=1, source_target_pairs={{0,8},{8,16},{16,24},{24,32},{32,40},{40,48},{48,56},{56,64},{64,7... | collective-permute-start | bytes 393224 | tf_op jit(solution)/shard_map/ppermute | solution.py:473
  42.5 14.9 %collective-permute-start.3 = (f32[16,16,128]{2,1,0:T(8,128)S(1)}, f32[16,16,128]{2,1,0:T(8,128)S(1)}, u32[]{:S(2)}, u32[]{:S(2)}) collective-permute-start(f32[16,16,128]{2,1,0:T(8,128)S(1)} %bitcast.22), channel_id=1, source_target_pairs={{8,0},{16,8},{24,16},{32,24},{40,32},{48,40},{56,48},{64,56},{72,6... | collective-permute-start | bytes 393224 | tf_op jit(solution)/shard_map/ppermute | solution.py:474
